TPU v7x, 512 devices: a whole 4x4x16 slice. The times are simulated.
512 devices in a mesh: mode: 64 (over y, z), rank: 8 (over x, core).
Axes of the slice: x: 4, y: 4, z: 16, core: 2. Of those that a mesh axis runs over, the one named last changes fastest.
Arguments:
- operator_cores: bfloat16 [2, 4, 4, 2048, 2048], P(None, None, None, 'mode'), may hold values from -0.26516504 to 0.26516504
- vector_cores: bfloat16 [2, 64, 64, 2048], P(None, 'rank', None, 'mode'), may hold values from -17 to 17
- left_gram: float32 [256, 256], replicated, may hold values from -330 to 330, as said below
- bases: float32 [3, 256, 64], replicated, may hold values from -0.375 to 0.375
Outputs:
- rounded_cores: float32 [2, 64, 2048, 64], P(None, None, ('mode', 'rank'))
- final_gram: float32 [256, 256], replicated
Inputs may be any that keep to these rules, and one draw needn't show every extreme that they name: left_gram is symmetric positive definite.
All inputs are finite; a program needn't handle non-finite values.
Results may differ from a plain program's by a relative error of at most 0.0028.
Values may be sent and summed in bfloat16 or wider, within the bound.
A program may use at most 64 MiB of HBM per device.

v0:
```python
import jax
import jax.numpy as jnp
from jax import lax
from jax.sharding import PartitionSpec as P

MODES = 2048
RANK = 256
HIGHEST_PRECISION = lax.Precision.HIGHEST


def solve_mixing(gram_now, basis):
    projected = jnp.dot(
        basis.T, gram_now, precision=HIGHEST_PRECISION, preferred_element_type=jnp.float32
    )
    reduced = jnp.dot(
        projected, basis, precision=HIGHEST_PRECISION, preferred_element_type=jnp.float32
    )
    reduced = 0.5 * (reduced + reduced.T)
    lower_factor = jnp.linalg.cholesky(reduced)
    return jax.scipy.linalg.cho_solve((lower_factor, True), projected)


def shards(operator_cores, vector_cores, left_gram, bases):
    gram_now = left_gram
    results = []
    core_count = operator_cores.shape[0]
    for core_index in range(core_count):
        mixing = solve_mixing(gram_now, bases[core_index])
        next_basis = bases[core_index + 1]
        operator_core = operator_cores[core_index]
        vector_core = vector_cores[core_index]
        local_rows = vector_core.shape[0]
        vector_width = vector_core.shape[1]
        operator_width = operator_core.shape[0]
        local_modes = operator_core.shape[2]
        gathered = lax.all_gather(vector_core, "mode", axis=2, tiled=True)
        product = jnp.einsum(
            "qsj,ptij->qpist", gathered, operator_core, preferred_element_type=jnp.float32
        )
        row_major = product.reshape(
            local_rows * operator_width, local_modes, vector_width * operator_width
        )
        row_major = row_major.astype(jnp.bfloat16)
        exchanged = lax.all_to_all(row_major, "rank", split_axis=1, concat_axis=0, tiled=True)
        widened = exchanged.astype(jnp.float32)
        weighted = jnp.einsum("ad,dib->aib", gram_now, widened, precision=HIGHEST_PRECISION)
        partial_gram = jnp.einsum("aib,aic->bc", widened, weighted, precision=HIGHEST_PRECISION) / (
            MODES * RANK
        )
        mixed = jnp.einsum("sa,aib->sib", mixing, widened, precision=HIGHEST_PRECISION)
        rounded_core = jnp.einsum("sib,bt->sit", mixed, next_basis, precision=HIGHEST_PRECISION)
        results.append(rounded_core)
        gram_now = lax.psum(partial_gram, ("mode", "rank"))
    return (jnp.stack(results), gram_now)


def solution(mesh):
    placed = (P(None, None, None, "mode", None), P(None, "rank", None, "mode"), P(), P())
    return jax.shard_map(
        shards,
        mesh=mesh,
        in_specs=placed,
        out_specs=(P(None, None, ("mode", "rank"), None), P()),
        check_vma=False,
    )
```

profile of v0, /device:TPU:4, one launch (start us, length us, event | category | flops | bytes accessed | tf_op | source)
XLA Modules:
  0.0 1263.4 jit_solution(10983501923882909832)
XLA Ops:
  7.2 0.9 fusion.62
  8.1 0.7 copy.55
  8.9 0.7 copy.56
  9.6 1.1 fusion.43
  10.7 1.0 fusion.41
  11.7 0.1 copy.28
  11.8 0.1 copy.29
  11.9 5.8 cholesky.44
  17.8 0.7 compare_reduce_fusion.1
  18.5 0.6 fusion.51
  19.1 4.9 custom-call.8
  24.0 0.3 fusion.58
  24.3 0.2 convolution_bitcast_fusion.6
  24.5 138.1 %all-gather.5.cloned.1.call-done = bf16[1,8,64,2048]{2,1,0,3:T(8,128)(2,1)} async-done(((bf16[1,8,64,32]{2,1,0,3:T(8,128)(2,1)}), bf16[1,8,64,2048]{2,1,0,3:T(8,128)(2,1)}) %all-gather.5.cloned.1.call-update) | async-done | bytes 2097168 | tf_op jit(solution)/shard_map/all_gather | solution.py:36
  162.6 4.5 copy.31
  167.1 3.9 fusion.23
  171.0 1.4 copy.32
  172.4 1.8 copy.33
  174.2 4.8 all-to-all-start
  179.0 128.4 %all-gather.7.cloned.1.call-done = bf16[1,8,64,2048]{2,1,0,3:T(8,128)(2,1)} async-done(((bf16[1,8,64,32]{2,1,0,3:T(8,128)(2,1)}), bf16[1,8,64,2048]{2,1,0,3:T(8,128)(2,1)}) %all-gather.7.cloned.1.call-update) | async-done | bytes 2097168 | tf_op jit(solution)/shard_map/all_gather | solution.py:36
  307.4 4.5 copy.41
  311.8 4.9 fusion.18
  316.8 2.9 copy.42
  319.7 1.8 copy.43
  321.4 4.8 all-to-all-start.1
  326.3 0.7 convolution_bitcast_fusion
  327.0 1.5 fusion.29
  328.5 0.2 all-reduce.5.cloned.1.call-start
  328.7 0.4 fusion.63
  329.1 4.3 all-to-all-done.1
  333.5 0.4 convolution_bitcast_fusion.4
  333.9 451.1 %all-reduce.3.cloned.1.call-done = f32[256,256]{1,0:T(8,128)} async-done(((f32[256,256]{1,0:T(8,128)}), f32[256,256]{1,0:T(8,128)}) %all-reduce.3.cloned.1.call-update) | async-done | bytes 262160 | tf_op jit(solution)/shard_map/psum | solution.py:53
  784.9 1.3 fusion.37
  786.2 0.2 fusion.39
  786.4 0.1 copy.38
  786.6 5.8 cholesky.55
  792.5 0.6 compare_reduce_fusion
  793.1 0.7 fusion.52
  793.8 4.9 custom-call.9
  798.7 0.3 fusion.34
  799.0 0.2 convolution_bitcast_fusion.5
  799.2 0.4 fusion.64
  799.6 0.6 fusion.30
  800.1 1.5 fusion.28
  801.7 0.4 convolution_bitcast_fusion.3
  802.1 0.9 copy.46
  802.9 452.2 %all-reduce.5.cloned.1.call-done = f32[256,256]{1,0:T(8,128)} async-done(((f32[256,256]{1,0:T(8,128)}), f32[256,256]{1,0:T(8,128)}) %all-reduce.5.cloned.1.call-update) | async-done | bytes 262160 | tf_op jit(solution)/shard_map/psum | solution.py:53
  1255.2 1.7 copy.59
  (24 shorter events, 0.5 us)
Async XLA Ops:
  7.2 2.4 copy-start
  7.2 155.4 %all-gather.5.cloned.1.call-start = ((), (), s32[]{:S(2)}) async-start(), calls=%async_computation.4 | async-start | bytes 4259840 | tf_op jit(solution)/shard_map/all_gather | solution.py:36
  8.8 298.6 %all-gather.7.cloned.1.call-start = ((), (), s32[]{:S(2)}) async-start(), calls=%async_computation.5 | async-start | bytes 4259840 | tf_op jit(solution)/shard_map/all_gather | solution.py:36
  174.2 147.2 %all-to-all-start = ((bf16[32,32,256]{2,0,1:T(8,128)(2,1)}), bf16[32,32,256]{2,0,1:T(8,128)(2,1)S(1)}, u32[]{:S(2)}, u32[]{:S(2)}) async-start(bf16[32,32,256]{2,0,1:T(8,128)(2,1)} %copy.33), calls=%async_computation | async-start | bytes 1048576 | tf_op jit(solution)/shard_map/all_to_all | solution.py:44
  321.4 12.0 all-to-all-start.1
  326.2 458.7 %all-reduce.3.cloned.1.call-start = ((), (), s32[]{:S(2)}) async-start(), calls=%async_computation.2 | async-start | bytes 524288 | tf_op jit(solution)/shard_map/psum | solution.py:53
  327.0 6.5 copy-start.2
  328.5 926.7 %all-reduce.5.cloned.1.call-start = ((), (), s32[]{:S(2)}) async-start(), calls=%async_computation.3 | async-start | bytes 524288 | tf_op jit(solution)/shard_map/psum | solution.py:53
  784.9 14.6 %copy-start.1 = (f32[256,256]{1,0:T(8,128)S(1)}, f32[256,256]{1,0:T(8,128)}, u32[]{:S(2)}) copy-start(f32[256,256]{1,0:T(8,128)} %all-reduce.3.cloned.1.call-done) | copy-start | bytes 786436
Sparse Core Ops, SparseCore 0:
  11.5 151.0 all-gather.4
  166.1 141.1 all-gather.6
  333.1 451.7 all-reduce.2
  801.8 453.3 all-reduce.4
where the time goes:
time: 1260 us
  waiting for transfers between devices  1170 us (93%)
  other arithmetic  24.2 us (2%)
  local copies, waits for them, and re-layouts  21.9 us (2%)
  matrix products  19.1 us (2%)
  between operations  14 us (1%)
    psum x2, waiting for transfers between devices, shards(): gram_now = lax.psum(partial_gram, ('mode', 'rank'))  903 us
    all_gather x2, waiting for transfers between devices, shards(): gathered = lax.all_gather(vector_core, 'mode', axis=2, tiled=True)  267 us
  transfers between devices with their start and end apart: 6, of which 5 were waited for; matrix products, arithmetic and copies ran while one was open for 4% of the time, Pallas kernels for 0%

commit v1 on v0

--- a/solution.py
+++ b/solution.py
@@ -6,6 +6,11 @@
 MODES = 2048
 RANK = 256
 HIGHEST_PRECISION = lax.Precision.HIGHEST
+
+
+def axis_by_axis(x, one, other):
+    partial = lax.psum(x, one)
+    return lax.psum(partial, other)
 
 
 def solve_mixing(gram_now, basis):
@@ -50,7 +55,7 @@
         mixed = jnp.einsum("sa,aib->sib", mixing, widened, precision=HIGHEST_PRECISION)
         rounded_core = jnp.einsum("sib,bt->sit", mixed, next_basis, precision=HIGHEST_PRECISION)
         results.append(rounded_core)
-        gram_now = lax.psum(partial_gram, ("mode", "rank"))
+        gram_now = axis_by_axis(partial_gram, "mode", "rank")
     return (jnp.stack(results), gram_now)
 
 

time: 1260 us -> 1020 us (0.81)
  the two profiles are of different devices: /device:TPU:4 before, /device:TPU:8 now
where the time goes in v1:
time: 1020 us
  waiting for transfers between devices  930 us (91%)
  other arithmetic  24.1 us (2%)
  local copies, waits for them, and re-layouts  21.9 us (2%)
  matrix products  20 us (2%)
  between operations  14.4 us (1%)
    psum x2, waiting for transfers between devices, axis_by_axis(): partial = lax.psum(x, one)  520 us
    all_gather x2, waiting for transfers between devices, shards(): gathered = lax.all_gather(vector_core, 'mode', axis=2, tiled=True)  266 us
    psum x2, waiting for transfers between devices, axis_by_axis(): return lax.psum(partial, other)  144 us
  transfers between devices with their start and end apart: 8, of which 6 were waited for; matrix products, arithmetic and copies ran while one was open for 4% of the time, Pallas kernels for 0%

profile of v1, /device:TPU:8, one launch (start us, length us, event | category | flops | bytes accessed | tf_op | source)
XLA Modules:
  0.0 1019.5 jit_solution(10153567072176903368)
XLA Ops:
  7.2 0.9 fusion.62
  8.1 0.7 copy.55
  8.9 0.7 copy.56
  9.6 1.1 fusion.43
  10.7 1.0 fusion.41
  11.7 0.1 copy.28
  11.9 5.8 cholesky.44
  17.8 0.6 compare_reduce_fusion.1
  18.5 0.6 fusion.51
  19.0 4.9 custom-call.8
  23.9 137.3 %all-gather.5.cloned.1.call-done = bf16[1,8,64,2048]{2,1,0,3:T(8,128)(2,1)} async-done(((bf16[1,8,64,32]{2,1,0,3:T(8,128)(2,1)}), bf16[1,8,64,2048]{2,1,0,3:T(8,128)(2,1)}) %all-gather.5.cloned.1.call-update) | async-done | bytes 2097168 | tf_op jit(solution)/shard_map/all_gather | solution.py:41
  161.2 4.5 copy.31
  165.7 3.9 fusion.23
  169.6 1.4 copy.32
  171.0 1.8 copy.33
  172.8 4.3 all-to-all-start
  177.1 128.9 %all-gather.7.cloned.1.call-done = bf16[1,8,64,2048]{2,1,0,3:T(8,128)(2,1)} async-done(((bf16[1,8,64,32]{2,1,0,3:T(8,128)(2,1)}), bf16[1,8,64,2048]{2,1,0,3:T(8,128)(2,1)}) %all-gather.7.cloned.1.call-update) | async-done | bytes 2097168 | tf_op jit(solution)/shard_map/all_gather | solution.py:41
  306.0 4.5 copy.41
  310.5 4.9 fusion.18
  315.4 2.9 copy.42
  318.3 1.8 copy.43
  320.0 4.3 all-to-all-start.1
  324.4 0.7 convolution_bitcast_fusion
  325.1 1.5 fusion.29
  326.7 0.3 fusion.58
  326.9 0.2 convolution_bitcast_fusion.6
  327.1 260.0 %all-reduce.5.cloned.1.call-done = f32[256,256]{1,0:T(8,128)} async-done(((f32[256,256]{1,0:T(8,128)}), f32[256,256]{1,0:T(8,128)}) %all-reduce.5.cloned.1.call-update) | async-done | bytes 262160 | tf_op jit(solution)/shard_map/psum | solution.py:12
  587.2 0.2 all-reduce.9.cloned.1.call-start
  587.4 0.4 fusion.63
  587.9 0.4 convolution_bitcast_fusion.4
  588.2 71.9 %all-reduce.7.cloned.1.call-done = f32[256,256]{1,0:T(8,128)} async-done(((f32[256,256]{1,0:T(8,128)}), f32[256,256]{1,0:T(8,128)}) %all-reduce.7.cloned.1.call-update) | async-done | bytes 262160 | tf_op jit(solution)/shard_map/psum | solution.py:13
  660.2 1.2 fusion.37
  661.4 0.2 fusion.39
  661.6 0.1 copy.38
  661.8 5.8 cholesky.55
  667.7 0.6 compare_reduce_fusion
  668.3 0.7 fusion.52
  669.0 4.9 custom-call.9
  673.9 0.3 fusion.34
  674.1 1.5 fusion.30
  675.7 1.5 fusion.28
  677.2 0.2 convolution_bitcast_fusion.5
  677.4 0.4 fusion.64
  677.8 260.2 %all-reduce.9.cloned.1.call-done = f32[256,256]{1,0:T(8,128)} async-done(((f32[256,256]{1,0:T(8,128)}), f32[256,256]{1,0:T(8,128)}) %all-reduce.9.cloned.1.call-update) | async-done | bytes 262160 | tf_op jit(solution)/shard_map/psum | solution.py:12
  938.0 0.4 convolution_bitcast_fusion.3
  938.4 0.9 copy.46
  939.3 71.7 %all-reduce.11.cloned.1.call-done = f32[256,256]{1,0:T(8,128)} async-done(((f32[256,256]{1,0:T(8,128)}), f32[256,256]{1,0:T(8,128)}) %all-reduce.11.cloned.1.call-update) | async-done | bytes 262160 | tf_op jit(solution)/shard_map/psum | solution.py:13
  1011.0 1.7 copy.61
  (28 shorter events, 0.7 us)
Async XLA Ops:
  7.2 2.4 copy-start
  7.2 154.1 %all-gather.5.cloned.1.call-start = ((), (), s32[]{:S(2)}) async-start(), calls=%async_computation.6 | async-start | bytes 4259840 | tf_op jit(solution)/shard_map/all_gather | solution.py:41
  8.8 297.2 %all-gather.7.cloned.1.call-start = ((), (), s32[]{:S(2)}) async-start(), calls=%async_computation.7 | async-start | bytes 4259840 | tf_op jit(solution)/shard_map/all_gather | solution.py:41
  172.8 147.2 %all-to-all-start = ((bf16[32,32,256]{2,0,1:T(8,128)(2,1)}), bf16[32,32,256]{2,0,1:T(8,128)(2,1)S(1)}, u32[]{:S(2)}, u32[]{:S(2)}) async-start(bf16[32,32,256]{2,0,1:T(8,128)(2,1)} %copy.33), calls=%async_computation | async-start | bytes 1048576 | tf_op jit(solution)/shard_map/all_to_all | solution.py:49
  320.0 267.7 %all-to-all-start.1 = ((bf16[32,32,256]{2,0,1:T(8,128)(2,1)}), bf16[32,32,256]{2,0,1:T(8,128)(2,1)S(1)}, u32[]{:S(2)}, u32[]{:S(2)}) async-start(bf16[32,32,256]{2,0,1:T(8,128)(2,1)} %copy.43), calls=%async_computation.1 | async-start | bytes 1048576 | tf_op jit(solution)/shard_map/all_to_all | solution.py:49
  324.3 262.8 %all-reduce.5.cloned.1.call-start = ((), (), s32[]{:S(2)}) async-start(), calls=%async_computation.2 | async-start | bytes 524288 | tf_op jit(solution)/shard_map/psum | solution.py:12
  325.1 262.7 %copy-start.1 = (f32[3,256,64]{1,2,0:T(8,128)S(1)}, f32[3,256,64]{1,2,0:T(8,128)}, u32[]{:S(2)}) copy-start(f32[3,256,64]{1,2,0:T(8,128)} %param.10) | copy-start | bytes 589828
  326.6 333.5 %all-reduce.7.cloned.1.call-start = ((), (), s32[]{:S(2)}) async-start(), calls=%async_computation.3 | async-start | bytes 524288 | tf_op jit(solution)/shard_map/psum | solution.py:13
  587.2 350.8 %all-reduce.9.cloned.1.call-start = ((), (), s32[]{:S(2)}) async-start(), calls=%async_computation.4 | async-start | bytes 524288 | tf_op jit(solution)/shard_map/psum | solution.py:12
  677.2 333.8 %all-reduce.11.cloned.1.call-start = ((), (), s32[]{:S(2)}) async-start(), calls=%async_computation.5 | async-start | bytes 524288 | tf_op jit(solution)/shard_map/psum | solution.py:13
Sparse Core Ops, SparseCore 0:
  11.5 149.6 all-gather.4
  164.8 141.1 all-gather.6
  329.1 257.9 all-reduce.4
  589.4 70.6 all-reduce.6
  677.3 260.6 all-reduce.8
  940.3 70.6 all-reduce.10
